TPU v7x, 32 devices: a whole 2x2x4 slice. The times are simulated.
32 devices in a mesh: grp: 4 (over x, core), mem: 4 (over z), pair: 2 (over y).
Axes of the slice: x: 2, y: 2, z: 4, core: 2. Of those that a mesh axis runs over, the one named last changes fastest.
Arguments:
- voltages: bfloat16 [1024, 2, 71680], P(('grp', 'mem'), 'pair'), may hold values from -6 to 6
- gain_table: float32 [64, 2, 1024], P(None, None, 'mem'), may hold values from -4.2 to 4.2
- gain_index: int32 [1024, 2], replicated, may hold values from 0 to 63
- cylinder_map: int32 [1024], replicated, may hold values from 0 to 1023, each once
- delays: int32 [32, 1024], replicated, may hold values from 0 to 31
- chan_map: int32 [1024], replicated, may hold values from 0 to 1023, each once
Outputs:
- dedispersed: float32 [2, 512, 32, 32], P('pair', ('grp', 'mem'))
Inputs may be any that keep to these rules, and one draw needn't show every extreme that they name: `cylinder_map`: each of 0 to 1023 appears once. `chan_map`: each of 0 to 1023 appears once.
All inputs are finite; a program needn't handle non-finite values.
Results may differ from a plain program's by a relative error of at most 0.011.
Values may be sent and summed in bfloat16 or wider, within the bound.
A program may use at most 128 MiB of HBM per device.

v0:
```python
import math
import jax
import jax.numpy as jnp
from jax import lax
from jax.sharding import PartitionSpec as P

NFFT = 2048
CHANS = 1024
TAPS = 4
CYL = 4
NS = 256
FEEDS = 1024
TIMES = 32
HIGHEST_PRECISION = lax.Precision.HIGHEST


def pfb_window(tap_count, length):
    offsets = jnp.arange(tap_count * length, dtype=jnp.float32) + 0.5
    shaped = jnp.sinc((offsets - tap_count * length / 2.0) / length)
    taper_term = 0.5 - 0.5 * jnp.cos(offsets * (2.0 * math.pi / (tap_count * length)))
    return (shaped * taper_term).reshape(tap_count, length)


def channel_table(length, start_col, columns):
    samples = jnp.arange(length, dtype=jnp.int32)[:, None]
    channels = start_col + jnp.arange(columns, dtype=jnp.int32)[None, :]
    turns_int = samples * channels % length
    angles = turns_int.astype(jnp.float32) * (2.0 * math.pi / length)
    return (jnp.cos(angles).astype(jnp.bfloat16), (-jnp.sin(angles)).astype(jnp.bfloat16))


def frame_signal(volt_rows, window):
    leading = volt_rows.shape[0]
    frames = volt_rows.reshape(leading, TIMES + TAPS - 1, NFFT).astype(jnp.float32)
    framed = frames[:, 0:TIMES] * window[0]
    for tap_index in range(1, TAPS):
        framed = framed + frames[:, tap_index : tap_index + TIMES] * window[tap_index]
    return framed.astype(jnp.bfloat16).reshape(leading * TIMES, NFFT)


def beam_table(length):
    samples = jnp.arange(length, dtype=jnp.int32).reshape(length, 1, 1)
    beam_index = (
        jnp.arange(length, dtype=jnp.int32).reshape(length // 2, 2).T.reshape(1, 2, length // 2)
    )
    turns_int = samples * beam_index % length
    angles = turns_int.astype(jnp.float32) * (2.0 * math.pi / length)
    cosine = jnp.cos(angles).astype(jnp.bfloat16)
    sine_part = jnp.sin(angles).astype(jnp.bfloat16)
    first_row = jnp.stack([cosine, -sine_part], axis=1)
    second_row = jnp.stack([sine_part, cosine], axis=1)
    return jnp.stack([first_row, second_row], axis=1)


def beam_power(ns_real, ns_imag, feed_total):
    cylinders = ns_real.shape[1]
    indices = jnp.arange(cylinders, dtype=jnp.int32)
    turns_int = indices[:, None] * indices[None, :] % cylinders
    angles = turns_int.astype(jnp.float32) * (2.0 * math.pi / cylinders)
    cosine = jnp.cos(angles)
    sine_table = jnp.sin(angles)
    beam_real = jnp.einsum(
        "ec,lchq->lehq", cosine, ns_real, precision=HIGHEST_PRECISION
    ) + jnp.einsum("ec,lchq->lehq", sine_table, ns_imag, precision=HIGHEST_PRECISION)
    beam_imag = jnp.einsum(
        "ec,lchq->lehq", cosine, ns_imag, precision=HIGHEST_PRECISION
    ) - jnp.einsum("ec,lchq->lehq", sine_table, ns_real, precision=HIGHEST_PRECISION)
    return (beam_real * beam_real + beam_imag * beam_imag) * (1.0 / feed_total)


def time_tables(length):
    indices = jnp.arange(length, dtype=jnp.int32)
    turns_int = indices[:, None] * indices[None, :] % length
    angles = turns_int.astype(jnp.float32) * (2.0 * math.pi / length)
    return (jnp.cos(angles), jnp.sin(angles))


def dedisperse(beam_data, delays, chan_map):
    beam_count = beam_data.shape[0]
    values = beam_data.astype(jnp.float32)
    centred = values - jnp.mean(values, axis=1, keepdims=True)
    cosine, sine_table = time_tables(TIMES)
    spec_real = jnp.einsum("btc,tk->bkc", centred, cosine, precision=HIGHEST_PRECISION).astype(
        jnp.bfloat16
    )
    spec_imag = (
        -jnp.einsum("btc,tk->bkc", centred, sine_table, precision=HIGHEST_PRECISION)
    ).astype(jnp.bfloat16)
    trial_delay = jnp.take(delays, chan_map, axis=1)
    block_waves = 8

    def trial_block(start_wave):
        wave_index = start_wave + jnp.arange(block_waves, dtype=jnp.int32)
        turns_int = wave_index[:, None, None] * trial_delay[None] % TIMES
        angles = turns_int.astype(jnp.float32) * (2.0 * math.pi / TIMES)
        phase_real = jnp.cos(angles).astype(jnp.bfloat16)
        phase_imag = (-jnp.sin(angles)).astype(jnp.bfloat16)
        part_real = lax.dynamic_slice_in_dim(spec_real, start_wave, block_waves, 1)
        part_imag = lax.dynamic_slice_in_dim(spec_imag, start_wave, block_waves, 1)
        trial_real = jnp.einsum(
            "bkc,kjc->bkj", part_real, phase_real, preferred_element_type=jnp.float32
        ) - jnp.einsum("bkc,kjc->bkj", part_imag, phase_imag, preferred_element_type=jnp.float32)
        trial_imag = jnp.einsum(
            "bkc,kjc->bkj", part_real, phase_imag, preferred_element_type=jnp.float32
        ) + jnp.einsum("bkc,kjc->bkj", part_imag, phase_real, preferred_element_type=jnp.float32)
        return (trial_real, trial_imag)

    starts = jnp.arange(0, TIMES, block_waves, dtype=jnp.int32)
    trial_real, trial_imag = lax.map(trial_block, starts)
    trial_count = trial_real.shape[-1]
    trial_real = jnp.moveaxis(trial_real, 0, 1).reshape(beam_count, TIMES, trial_count)
    trial_imag = jnp.moveaxis(trial_imag, 0, 1).reshape(beam_count, TIMES, trial_count)
    scale_out = 1.0 / (TIMES * math.sqrt(CHANS))
    series = jnp.einsum(
        "bkj,kt->bjt", trial_real, cosine, precision=HIGHEST_PRECISION
    ) - jnp.einsum("bkj,kt->bjt", trial_imag, sine_table, precision=HIGHEST_PRECISION)
    return series * scale_out


def local(voltages, gain_table, gain_index, cylinder_map, delays, chan_map):
    local_feeds = voltages.shape[0]
    window = pfb_window(TAPS, NFFT)
    framed = frame_signal(voltages.reshape(local_feeds, voltages.shape[2]), window)
    scale_dft = 1.0 / math.sqrt(NFFT)
    block_cols = min(256, CHANS)

    def fill_block(block_index, spectra):
        start_col = block_index * block_cols
        cos_table, sin_table = channel_table(NFFT, start_col, block_cols)
        real_part = jnp.dot(framed, cos_table, preferred_element_type=jnp.float32) * scale_dft
        imag_part = jnp.dot(framed, sin_table, preferred_element_type=jnp.float32) * scale_dft
        stacked = jnp.stack([real_part, imag_part], axis=0).astype(jnp.bfloat16)
        stacked = stacked.reshape(2, local_feeds, TIMES, block_cols)
        return lax.dynamic_update_slice_in_dim(spectra, stacked, start_col, 3)

    spectra = lax.fori_loop(
        0, CHANS // block_cols, fill_block, jnp.zeros((2, local_feeds, TIMES, CHANS), jnp.bfloat16)
    )
    grp_count = lax.axis_size("grp")
    mem_count = lax.axis_size("mem")
    owners = cylinder_map // local_feeds
    slot_rows = (
        owners % mem_count * grp_count + owners // mem_count
    ) * local_feeds + cylinder_map % local_feeds
    table_beams = beam_table(NS)
    half_beams = CYL * (NS // 2)
    received = lax.all_to_all(
        lax.all_to_all(spectra, "grp", split_axis=2, concat_axis=1, tiled=True),
        "mem",
        split_axis=3,
        concat_axis=1,
        tiled=True,
    )
    polarization = lax.axis_index("pair")
    gain_column = lax.dynamic_index_in_dim(gain_index, polarization, 1, keepdims=False)
    gain_values = jnp.take(gain_table, jnp.take(gain_column, cylinder_map), axis=0)
    gain_real = gain_values[:, 0][:, None, :]
    gain_imag = gain_values[:, 1][:, None, :]
    ordered = jnp.take(received, slot_rows, axis=1)
    volt_real = ordered[0].astype(jnp.float32)
    volt_imag = ordered[1].astype(jnp.float32)
    cal_real = volt_real * gain_real - volt_imag * gain_imag
    cal_imag = volt_real * gain_imag + volt_imag * gain_real
    cal_grid = jnp.stack([cal_real, cal_imag], axis=0).astype(jnp.bfloat16)
    frame_local = cal_grid.shape[2]
    chan_local = cal_grid.shape[3]
    cal_grid = cal_grid.reshape(2, CYL, NS, frame_local * chan_local)
    ns_beams = jnp.einsum(
        "rcnq,nrsah->sachq", cal_grid, table_beams, preferred_element_type=jnp.float32
    )
    powers = beam_power(ns_beams[0], ns_beams[1], FEEDS)
    summed = lax.psum_scatter(powers, "pair", scatter_dimension=0, tiled=True)
    intensity = summed.astype(jnp.bfloat16).reshape(half_beams, frame_local, chan_local)
    beam_data = lax.all_to_all(
        lax.all_to_all(intensity, "grp", split_axis=0, concat_axis=1, tiled=True),
        "mem",
        split_axis=0,
        concat_axis=2,
        tiled=True,
    )
    series = dedisperse(beam_data, delays, chan_map)
    return series[None]


def solution(mesh):
    return jax.shard_map(
        local,
        mesh=mesh,
        in_specs=(P(("grp", "mem"), "pair", None), P(None, None, "mem"), P(), P(), P(), P()),
        out_specs=P("pair", ("grp", "mem"), None, None),
        check_vma=False,
    )
```

profile of v0, /device:TPU:0, one launch (start us, length us, event | category | flops | bytes accessed | tf_op | source)
XLA Modules:
  0.0 966.5 jit_solution(392109306165076913)
XLA Ops:
  6.7 12.8 %reshape.199 = f32[64,35,2048]{2,1,0:T(8,128)} reshape(bf16[64,1,71680]{2,0,1:T(8,128)(2,1)} %param.10) | data formatting | bytes 27525120 | tf_op jit(solution)/shard_map/convert_element_type | solution.py:34
  19.5 31.6 %fusion.50 = bf16[64,32,2048]{2,1,0:T(8,128)(2,1)} fusion(f32[64,35,2048]{2,1,0:T(8,128)} %reshape.199, f32[2048]{0:T(1024)S(1)} %get-tuple-element.263, f32[2048]{0:T(1024)S(1)} %get-tuple-element.264, f32[2048]{0:T(1024)S(1)} %get-tuple-element.265, f32[2048]{0:T(1024)S(1)} %get-tuple-element.262), kind=kLoop, calls=%fused_computation.75 | loop fusion | flops 33554432 | bytes 75530240 | tf_op jit(solution)/shard_map/convert_element_type | solution.py:38
  51.1 4.3 broadcast_in_dim.83.clone
  55.4 129.2 %while.29 = (s32[]{:T(128)}, bf16[2,64,32,1024]{3,1,0,2:T(8,128)(2,1)}, bf16[2048,2048]{1,0:T(8,128)(2,1)}, s32[]{:T(128)}, s32[]{:T(128)}, /*index=5*/s32[]{:T(128)}, s32[]{:T(128)}) while((s32[]{:T(128)}, bf16[2,64,32,1024]{3,1,0,2:T(8,128)(2,1)}, bf16[2048,2048]{1,0:T(8,128)(2,1)}, s32[]{:T(128)}, s32[]{:T(128)}, /*index=5*/s32[]{:T(128)}, ...), condition=%wide.region_1.2_spmd, body=%wide.region_0.1_spmd.sunk | while | flops 4314365952 | bytes 31460484 | solution.py:136
  55.4 13.2 %fusion.217 = bf16[2048,256]{0,1:T(8,128)(2,1)S(1)} fusion(bf16[2048,2048]{1,0:T(8,128)(2,1)} %get-tuple-element.353, s32[256]{0:T(256)S(1)} %iota_add_fusion.6), kind=kOutput, calls=%fused_computation.11.clone.1 | convolution fusion | flops 2156920832 | bytes 9438208 | tf_op jit(solution)/shard_map/while/body/eval_jaxpr/dot_general | solution.py:131
  69.2 13.2 %fusion.218 = bf16[2048,256]{0,1:T(8,128)(2,1)S(1)} fusion(bf16[2048,2048]{1,0:T(8,128)(2,1)} %get-tuple-element.353, s32[256]{0:T(256)S(1)} %iota_add_fusion.6), kind=kOutput, calls=%fused_computation.12.clone.1 | convolution fusion | flops 2156396544 | bytes 9438208 | tf_op jit(solution)/shard_map/while/body/eval_jaxpr/dot_general | solution.py:130
  85.1 2.6 copy_dynamic-update-slice_fusion.2
  87.8 13.2 %fusion.217 = bf16[2048,256]{0,1:T(8,128)(2,1)S(1)} fusion(bf16[2048,2048]{1,0:T(8,128)(2,1)} %get-tuple-element.353, s32[256]{0:T(256)S(1)} %iota_add_fusion.6), kind=kOutput, calls=%fused_computation.11.clone.1 | convolution fusion | flops 2156920832 | bytes 9438208 | tf_op jit(solution)/shard_map/while/body/eval_jaxpr/dot_general | solution.py:131
  101.5 13.2 %fusion.218 = bf16[2048,256]{0,1:T(8,128)(2,1)S(1)} fusion(bf16[2048,2048]{1,0:T(8,128)(2,1)} %get-tuple-element.353, s32[256]{0:T(256)S(1)} %iota_add_fusion.6), kind=kOutput, calls=%fused_computation.12.clone.1 | convolution fusion | flops 2156396544 | bytes 9438208 | tf_op jit(solution)/shard_map/while/body/eval_jaxpr/dot_general | solution.py:130
  117.5 2.6 copy_dynamic-update-slice_fusion.2
  120.1 13.2 %fusion.217 = bf16[2048,256]{0,1:T(8,128)(2,1)S(1)} fusion(bf16[2048,2048]{1,0:T(8,128)(2,1)} %get-tuple-element.353, s32[256]{0:T(256)S(1)} %iota_add_fusion.6), kind=kOutput, calls=%fused_computation.11.clone.1 | convolution fusion | flops 2156920832 | bytes 9438208 | tf_op jit(solution)/shard_map/while/body/eval_jaxpr/dot_general | solution.py:131
  133.8 13.2 %fusion.218 = bf16[2048,256]{0,1:T(8,128)(2,1)S(1)} fusion(bf16[2048,2048]{1,0:T(8,128)(2,1)} %get-tuple-element.353, s32[256]{0:T(256)S(1)} %iota_add_fusion.6), kind=kOutput, calls=%fused_computation.12.clone.1 | convolution fusion | flops 2156396544 | bytes 9438208 | tf_op jit(solution)/shard_map/while/body/eval_jaxpr/dot_general | solution.py:130
  149.8 2.6 copy_dynamic-update-slice_fusion.2
  152.4 13.2 %fusion.217 = bf16[2048,256]{0,1:T(8,128)(2,1)S(1)} fusion(bf16[2048,2048]{1,0:T(8,128)(2,1)} %get-tuple-element.353, s32[256]{0:T(256)S(1)} %iota_add_fusion.6), kind=kOutput, calls=%fused_computation.11.clone.1 | convolution fusion | flops 2156920832 | bytes 9438208 | tf_op jit(solution)/shard_map/while/body/eval_jaxpr/dot_general | solution.py:131
  166.1 13.2 %fusion.218 = bf16[2048,256]{0,1:T(8,128)(2,1)S(1)} fusion(bf16[2048,2048]{1,0:T(8,128)(2,1)} %get-tuple-element.353, s32[256]{0:T(256)S(1)} %iota_add_fusion.6), kind=kOutput, calls=%fused_computation.12.clone.1 | convolution fusion | flops 2156396544 | bytes 9438208 | tf_op jit(solution)/shard_map/while/body/eval_jaxpr/dot_general | solution.py:130
  182.1 2.5 copy_dynamic-update-slice_fusion.2
  184.6 101.4 %all_to_all.63 = bf16[2,64,32,1024]{3,1,0,2:T(8,128)(2,1)} all-to-all(bf16[2,64,32,1024]{3,1,0,2:T(8,128)(2,1)} %get-tuple-element.185), channel_id=1, replica_groups=mesh['grp'=4,'mem'=4,'pair'=2] {'grp'}, dimensions={2} | all-to-all | bytes 16777216 | tf_op jit(solution)/shard_map/all_to_all | solution.py:148
  286.0 11.9 %copy.114 = bf16[2,4,64,8,1024]{4,3,2,1,0:T(8,128)(2,1)} copy(bf16[2,4,64,8,1024]{4,2,0,3,1:T(8,128)(2,1)} %bitcast.163) | data formatting | bytes 16777216 | tf_op jit(solution)/shard_map/all_to_all | solution.py:148
  297.9 13.4 %copy.115 = bf16[2,256,8,1024]{1,2,0,3:T(8,128)(2,1)} copy(bf16[2,256,8,1024]{3,2,1,0:T(8,128)(2,1)} %bitcast.164) | data formatting | bytes 16777216 | tf_op jit(solution)/shard_map/all_to_all | solution.py:148
  311.3 5.8 all-to-all-start.1
  317.4 4.5 gather_fusion.2
  322.0 4.1 gather_fusion.3
  328.6 3.7 broadcast_select_fusion
  334.1 166.8 %all-to-all-done.1 = bf16[2,256,8,1024]{1,2,0,3:T(8,128)(2,1)} async-done(((bf16[2,256,8,1024]{1,2,0,3:T(8,128)(2,1)}), bf16[2,256,8,1024]{1,2,0,3:T(8,128)(2,1)}, u32[]{:S(2)}, u32[]{:S(2)}) %all-to-all-start.1) | async-done | bytes 8388640 | tf_op jit(solution)/shard_map/all_to_all | solution.py:147
  500.9 15.9 %copy.117 = bf16[2,4,256,8,256]{4,3,2,1,0:T(8,128)(2,1)} copy(bf16[2,4,256,8,256]{2,3,0,4,1:T(8,128)(2,1)} %bitcast.23) | data formatting | bytes 16777216 | tf_op jit(solution)/shard_map/all_to_all | solution.py:147
  516.8 13.0 %gather_fusion.1 = bf16[1024,2,8,256]{3,2,1,0:T(8,128)(2,1)} fusion(bf16[2,1024,8,256]{3,2,1,0:T(8,128)(2,1)} %bitcast.162, s32[1024]{0:T(1024)S(1)} %broadcast_clamp_fusion.1), kind=kCustom, calls=%fused_computation.1 | custom fusion | bytes 16781312 | tf_op jit(solution)/shard_map/jit(_take)/gather | solution.py:159
  529.8 6.1 select_bitcast_fusion
  535.9 4.8 fusion.54
  540.7 7.4 stack.48
  548.1 7.7 stack.49
  555.8 13.7 %fusion.68 = f32[2,2,4,128,2048]{4,3,2,1,0:T(8,128)} fusion(bf16[1,4,256,2048]{3,2,0,1:T(8,128)(2,1)} %stack.49, bf16[1,4,256,2048]{3,2,0,1:T(8,128)(2,1)} %stack.48, bf16[256,1,2,2,128]{0,4,1,3,2:T(8,128)(2,1)S(1)} %get-tuple-element.261, bf16[256,1,2,2,128]{0,4,1,3,2:T(8,128)(2,1)S(1)} %get-tuple-element.260), kind=kOutput, calls=%fused_computation.105 | convolution fusion | flops 4312793088 | bytes 25690112 | tf_op jit(solution)/shard_map/rcnq,nrsah->sachq/dot_general | solution.py:168
  569.5 6.5 slice_bitcast_fusion.1
  576.0 18.4 %fusion.60 = f32[2,128,2048,4]{2,3,1,0:T(4,128)} fusion(f32[2,4,128,2048]{3,2,1,0:T(8,128)S(1)} %get-tuple-element.255), kind=kOutput, calls=%fused_computation.97 | convolution fusion | flops 100663520 | bytes 16777216 | tf_op jit(solution)/shard_map/ec,lchq->lehq/dot_general | solution.py:65
  594.4 19.0 %fusion.62 = f32[2,128,2048,4]{2,3,1,0:T(4,128)} fusion(f32[2,4,128,2048]{3,2,1,0:T(8,128)S(1)} %get-tuple-element.255), kind=kOutput, calls=%fused_computation.99 | convolution fusion | flops 100663520 | bytes 16777216 | tf_op jit(solution)/shard_map/ec,lchq->lehq/dot_general | solution.py:64
  613.4 18.5 %fusion.64 = f32[2,128,2048,4]{2,3,1,0:T(4,128)} fusion(f32[2,4,128,2048]{3,2,1,0:T(8,128)S(1)} %get-tuple-element.254), kind=kOutput, calls=%fused_computation.101 | convolution fusion | flops 100663520 | bytes 16777216 | tf_op jit(solution)/shard_map/ec,lchq->lehq/dot_general | solution.py:67
  631.8 30.1 %multiply_bitcast_fusion = f32[2,4,128,2048]{3,1,2,0:T(4,128)} fusion(f32[2,128,2048,4]{2,3,1,0:T(4,128)} %fusion.60, f32[2,128,2048,4]{2,3,1,0:T(4,128)} %fusion.64, f32[2,128,2048,4]{2,3,1,0:T(4,128)} %fusion.62, f32[2,4,128,2048]{3,2,1,0:T(8,128)} %copy-done.2), kind=kOutput, calls=%fused_computation.96 | convolution fusion | flops 113246432 | bytes 41943040 | tf_op jit(solution)/shard_map/ec,lchq->lehq/dot_general | solution.py:62
  661.9 11.5 %copy.122 = f32[2,4,128,2048]{3,2,1,0:T(8,128)} copy(f32[2,4,128,2048]{3,1,2,0:T(4,128)} %multiply_bitcast_fusion) | data formatting | bytes 16777216 | tf_op jit(solution)/shard_map/mul | solution.py:68
  673.5 97.9 %reduce-scatter.2.cloned.1.call-done = f32[1,4,128,2048]{3,2,1,0:T(8,128)} async-done(((f32[2,4,128,2048]{3,2,1,0:T(8,128)}), f32[1,4,128,2048]{3,2,1,0:T(8,128)}) %reduce-scatter.2.cloned.1.call-update) | async-done | bytes 4194320 | tf_op jit(solution)/shard_map/reduce_scatter | solution.py:172
  771.4 2.5 convert_element_type.195
  774.6 28.2 %all_to_all.64 = bf16[512,8,256]{2,1,0:T(8,128)(2,1)S(1)} all-to-all(bf16[512,8,256]{2,1,0:T(8,128)(2,1)S(1)} %bitcast.169), channel_id=1, replica_groups=mesh['grp'=4,'mem'=4,'pair'=2] {'grp'}, dimensions={0} | all-to-all | bytes 4194304 | tf_op jit(solution)/shard_map/all_to_all | solution.py:175
  804.4 4.6 all-to-all-start.3
  809.2 2.8 gather_fusion
  812.5 44.4 %all-to-all-done.3 = bf16[128,32,256]{2,1,0:T(8,128)(2,1)S(1)} async-done(((bf16[128,32,256]{2,1,0:T(8,128)(2,1)}), bf16[128,32,256]{2,1,0:T(8,128)(2,1)S(1)}, u32[]{:S(2)}, u32[]{:S(2)}) %all-to-all-start.3) | async-done | bytes 2097184 | tf_op jit(solution)/shard_map/all_to_all | solution.py:174
  858.2 4.1 fusion.75
  862.3 5.1 convert_bitcast_fusion
  867.4 88.8 %while.30 = (s32[]{:T(128)}, f32[4,32,8,32]{1,3,2,0:T(8,128)S(1)}, f32[4,32,8,32]{1,3,2,0:T(8,128)S(1)}, s32[4]{0:T(128)S(1)}, s32[32,1024]{1,0:T(8,128)S(1)}, /...) while((s32[]{:T(128)}, f32[4,32,8,32]{1,3,2,0:T(8,128)S(1)}, ...), condition=%wide.region_5.6_spmd, body=%wide.region_4.5_spmd.sunk | while | flops 83378192 | bytes 5309699 | solution.py:109
  870.1 1.7 constant_dynamic-slice_fusion.4
  872.4 4.4 fusion.225
  876.8 4.3 fusion.226
  881.1 4.3 fusion.223
  885.4 4.4 fusion.224
  892.3 1.7 constant_dynamic-slice_fusion.4
  894.6 4.4 fusion.225
  899.0 4.3 fusion.226
  903.3 4.3 fusion.223
  907.6 4.4 fusion.224
  916.8 4.4 fusion.225
  921.2 4.3 fusion.226
  925.5 4.3 fusion.223
  929.8 4.4 fusion.224
  938.8 4.4 fusion.225
  943.2 4.3 fusion.226
  947.5 4.3 fusion.223
  951.8 4.4 fusion.224
  (77 shorter events, 33.1 us)
Async XLA Ops:
  6.5 315.5 %copy-start = (f32[64,2,256]{2,1,0:T(2,128)S(1)}, f32[64,2,256]{2,1,0:T(2,128)}, u32[]{:S(2)}) copy-start(f32[64,2,256]{2,1,0:T(2,128)} %param.11) | copy-start | bytes 393220
  311.3 6.0 copy-start.8
  311.3 6.1 copy-start.6
  311.3 189.5 %all-to-all-start.1 = ((bf16[2,256,8,1024]{1,2,0,3:T(8,128)(2,1)}), bf16[2,256,8,1024]{1,2,0,3:T(8,128)(2,1)}, u32[]{:S(2)}, u32[]{:S(2)}) async-start(bf16[2,256,8,1024]{1,2,0,3:T(8,128)(2,1)} %copy.115), calls=%async_computation.1 | async-start | bytes 16777216 | tf_op jit(solution)/shard_map/all_to_all | solution.py:147
  317.1 454.2 %reduce-scatter.2.cloned.1.call-start = ((), (), s32[]{:S(2)}) async-start(), calls=%async_computation.5 | async-start | bytes 12582912 | tf_op jit(solution)/shard_map/reduce_scatter | solution.py:172
  576.0 37.4 %copy-start.2 = (f32[2,4,128,2048]{3,2,1,0:T(8,128)}, f32[2,4,128,2048]{3,2,1,0:T(8,128)S(1)}, u32[]{:S(2)}) copy-start(f32[2,4,128,2048]{3,2,1,0:T(8,128)S(1)} %get-tuple-element.254) | copy-start | bytes 25165828
  773.9 35.1 %copy-start.5 = (s32[32,1024]{1,0:T(8,128)S(1)}, s32[32,1024]{1,0:T(8,128)}, u32[]{:S(2)}) copy-start(s32[32,1024]{1,0:T(8,128)} %param.14) | copy-start | bytes 393220
  773.9 35.3 %copy-start.7 = (s32[1024]{0:T(1024)S(1)}, s32[1024]{0:T(1024)}, u32[]{:S(2)}) copy-start(s32[1024]{0:T(1024)} %param.15) | copy-start | bytes 12292
  804.4 52.4 %all-to-all-start.3 = ((bf16[128,32,256]{2,1,0:T(8,128)(2,1)}), bf16[128,32,256]{2,1,0:T(8,128)(2,1)S(1)}, u32[]{:S(2)}, u32[]{:S(2)}) async-start(bf16[128,32,256]{2,1,0:T(8,128)(2,1)} %bitcast.168), calls=%async_computation.4 | async-start | bytes 4194304 | tf_op jit(solution)/shard_map/all_to_all | solution.py:174
  857.4 10.0 %copy-start.3 = (f32[4,32,8,32]{1,3,2,0:T(8,128)S(1)}, f32[4,32,8,32]{1,3,2,0:T(8,128)}, u32[]{:S(2)}) copy-start(f32[4,32,8,32]{1,3,2,0:T(8,128)} %custom-call.8) | copy-start | bytes 393220
  857.4 10.0 %copy-start.4 = (f32[4,32,8,32]{1,3,2,0:T(8,128)S(1)}, f32[4,32,8,32]{1,3,2,0:T(8,128)}, u32[]{:S(2)}) copy-start(f32[4,32,8,32]{1,3,2,0:T(8,128)} %custom-call.9) | copy-start | bytes 393220
  956.2 3.2 copy-start.1
Sparse Core Ops, SparseCore 0:
  673.6 97.7 reduce-scatter.1
where the time goes:
time: 977 us; the launch traced here: 966 us
  waiting for transfers between devices  309 us (32%)
  matrix products  286 us (29%)
  local copies, waits for them, and re-layouts  148 us (15%)
  blocking collectives  130 us (13%)
  other arithmetic  60.5 us (6%)
  between operations  13.9 us (1%)
  starting transfers between devices  10.6 us (1%)
    all_to_all x1, waiting for transfers between devices, local(): lax.all_to_all(lax.all_to_all(spectra, 'grp', split_axis=2, concat_axis=1...  167 us
    all_to_all x1, blocking collectives, local(): lax.all_to_all(spectra, 'grp', split_axis=2, concat_axis=1, tiled=True)  101 us
    reduce_scatter x1, waiting for transfers between devices, local(): summed = lax.psum_scatter(powers, 'pair', scatter_dimension=0, tiled=True)  97.9 us
    dot_general x4, matrix products, fill_block(): jnp.dot(framed, cos_table, preferred_element_type=jnp.float32) * scale_dft  53 us
    dot_general x4, matrix products, fill_block(): jnp.dot(framed, sin_table, preferred_element_type=jnp.float32) * scale_dft  52.8 us
    all_to_all x1, waiting for transfers between devices, local(): lax.all_to_all(lax.all_to_all(intensity, 'grp', split_axis=0, concat_axis...  44.4 us
    convert_element_type x1, other arithmetic, frame_signal(): return framed.astype(jnp.bfloat16).reshape(leading * TIMES, NFFT)  31.6 us
    dot_general x1, matrix products, beam_power(): jnp.einsum('ec,lchq->lehq', cosine, ns_real, precision=HIGHEST_PRECISION)  30.1 us
  transfers between devices with their start and end apart: 3, of which 3 were waited for; matrix products, arithmetic and copies ran while one was open for 2% of the time, Pallas kernels for 0%

commit v1 on v0

--- a/solution.py
+++ b/solution.py
@@ -12,6 +12,28 @@
 FEEDS = 1024
 TIMES = 32
 HIGHEST_PRECISION = lax.Precision.HIGHEST
+
+
+def cut_along(value, dim, devices):
+    before, after = (value.shape[:dim], value.shape[dim + 1 :])
+    return jnp.moveaxis(value.reshape(*before, devices, -1, *after), dim, 0)
+
+
+def in_order(tiles, dim):
+    tiles = jnp.moveaxis(tiles, 0, dim)
+    lengths = tiles.shape
+    return tiles.reshape(*lengths[:dim], lengths[dim] * lengths[dim + 1], *lengths[dim + 2 :])
+
+
+def exchange_directly(x, axis, split_dim, concat_dim):
+    count, position = (lax.axis_size(axis), lax.axis_index(axis))
+    blocks = cut_along(x, split_dim, count)
+    outs = [blocks[position]]
+    for step in range(1, count):
+        sent = blocks[(position + step) % count]
+        outs.append(lax.ppermute(sent, axis, [(i, (i + step) % count) for i in range(count)]))
+    blocks = jnp.stack(outs)[(position - jnp.arange(count)) % count]
+    return in_order(blocks, concat_dim)
 
 
 def pfb_window(tap_count, length):
@@ -145,11 +167,7 @@
     table_beams = beam_table(NS)
     half_beams = CYL * (NS // 2)
     received = lax.all_to_all(
-        lax.all_to_all(spectra, "grp", split_axis=2, concat_axis=1, tiled=True),
-        "mem",
-        split_axis=3,
-        concat_axis=1,
-        tiled=True,
+        exchange_directly(spectra, "grp", 2, 1), "mem", split_axis=3, concat_axis=1, tiled=True
     )
     polarization = lax.axis_index("pair")
     gain_column = lax.dynamic_index_in_dim(gain_index, polarization, 1, keepdims=False)

time: 977 us -> 986 us (level)
  blocking collectives: 130 us -> 28.2 us
  waiting for transfers between devices: 309 us -> 395 us
  other arithmetic: 60.5 us -> 70.7 us
  local copies, waits for them, and re-layouts: 148 us -> 158 us
    all_to_all x1 -> x0, blocking collectives: 101 us -> none  [local(): lax.all_to_all(spectra, 'grp', split_axis=2, concat_axis=1, tiled=True)]
    ppermute x0 -> x3, waiting for transfers between devices: none -> 85.3 us  [exchange_directly(): lax.ppermute(sent, axis, [(i, (i + step) % count) for i in range(count)])]
    all_to_all x3 -> x1, local copies, waits for them, and re-layouts: 41.3 us -> 15.9 us  [local(): lax.all_to_all(exchange_directly(spectra, 'grp', 2, 1), 'mem', split_axis...]
    gather x0 -> x3, local copies, waits for them, and re-layouts: none -> 13.8 us  [exchange_directly(): blocks = jnp.stack(outs)[(position - jnp.arange(count)) % count]]
    reshape x0 -> x1, local copies, waits for them, and re-layouts: none -> 13.4 us  [in_order(): tiles.reshape(*lengths[:dim], lengths[dim] * lengths[dim + 1], *lengths[d...]
    transpose x0 -> x1, local copies, waits for them, and re-layouts: none -> 11.9 us  [in_order(): tiles = jnp.moveaxis(tiles, 0, dim)]
    dynamic_update_slice x4 -> x0, local copies, waits for them, and re-layouts: 10.3 us -> none  [fill_block(): return lax.dynamic_update_slice_in_dim(spectra, stacked, start_col, 3)]
  transfers between devices with their start and end apart: 3 -> 6, of which waited for: 3 -> 6; matrix products, arithmetic and copies ran while one was open for 2% -> 2% of each run, Pallas kernels for 0% -> 0%
where the time goes in v1:
time: 986 us; the launch traced here: 975 us
  waiting for transfers between devices  395 us (40%)
  matrix products  286 us (29%)
  local copies, waits for them, and re-layouts  158 us (16%)
  other arithmetic  70.7 us (7%)
  blocking collectives  28.2 us (3%)
  starting transfers between devices  15.6 us (2%)
  between operations  14.2 us (1%)
    all_to_all x1, waiting for transfers between devices, local(): lax.all_to_all(exchange_directly(spectra, 'grp', 2, 1), 'mem', split_axis...  167 us
    reduce_scatter x1, waiting for transfers between devices, local(): summed = lax.psum_scatter(powers, 'pair', scatter_dimension=0, tiled=True)  97.7 us
    ppermute x3, waiting for transfers between devices, exchange_directly(): lax.ppermute(sent, axis, [(i, (i + step) % count) for i in range(count)])  85.3 us
    dot_general x4, matrix products, fill_block(): jnp.dot(framed, cos_table, preferred_element_type=jnp.float32) * scale_dft  53 us
    dot_general x4, matrix products, fill_block(): jnp.dot(framed, sin_table, preferred_element_type=jnp.float32) * scale_dft  52.8 us
    all_to_all x1, waiting for transfers between devices, local(): lax.all_to_all(lax.all_to_all(intensity, 'grp', split_axis=0, concat_axis...  44.4 us
    convert_element_type x1, other arithmetic, frame_signal(): return framed.astype(jnp.bfloat16).reshape(leading * TIMES, NFFT)  31.6 us
    dot_general x1, matrix products, beam_power(): jnp.einsum('ec,lchq->lehq', cosine, ns_real, precision=HIGHEST_PRECISION)  30.1 us
  transfers between devices with their start and end apart: 6, of which 6 were waited for; matrix products, arithmetic and copies ran while one was open for 2% of the time, Pallas kernels for 0%

profile of v1, /device:TPU:0, one launch (start us, length us, event | category | flops | bytes accessed | tf_op | source)
XLA Modules:
  0.0 975.2 jit_solution(5674359293804538179)
XLA Ops:
  6.7 12.8 %reshape.263 = f32[64,35,2048]{2,1,0:T(8,128)} reshape(bf16[64,1,71680]{2,0,1:T(8,128)(2,1)} %param.10) | data formatting | bytes 27525120 | tf_op jit(solution)/shard_map/convert_element_type | solution.py:56
  19.5 31.6 %fusion.50 = bf16[64,32,2048]{2,1,0:T(8,128)(2,1)} fusion(f32[64,35,2048]{2,1,0:T(8,128)} %reshape.263, f32[2048]{0:T(1024)S(1)} %get-tuple-element.269, f32[2048]{0:T(1024)S(1)} %get-tuple-element.270, f32[2048]{0:T(1024)S(1)} %get-tuple-element.271, f32[2048]{0:T(1024)S(1)} %get-tuple-element.268), kind=kLoop, calls=%fused_computation.76 | loop fusion | flops 33554432 | bytes 75530240 | tf_op jit(solution)/shard_map/convert_element_type | solution.py:60
  51.1 4.3 broadcast_in_dim.84
  55.5 116.6 %while.29 = (s32[]{:T(128)}, bf16[2,64,32,1024]{3,2,1,0:T(8,128)(2,1)}, bf16[2048,2048]{1,0:T(8,128)(2,1)}, s32[]{:T(128)}, s32[]{:T(128)}, /*index=5*/s32[]{:T(128)}, s32[]{:T(128)}) while((s32[]{:T(128)}, bf16[2,64,32,1024]{3,2,1,0:T(8,128)(2,1)}, bf16[2048,2048]{1,0:T(8,128)(2,1)}, s32[]{:T(128)}, s32[]{:T(128)}, /*index=5*/s32[]{:T(128)}, ...), condition=%wide.region_1.2_spmd, body=%wide.region_0.1_spmd.sunk | while | flops 4317511680 | bytes 27266180 | solution.py:158
  55.5 13.2 %fusion.220 = bf16[2048,256]{0,1:T(8,128)(2,1)S(1)} fusion(bf16[2048,2048]{1,0:T(8,128)(2,1)} %get-tuple-element.359, s32[256]{0:T(256)S(1)} %iota_add_fusion.6), kind=kOutput, calls=%fused_computation.13.clone.1 | convolution fusion | flops 2156920832 | bytes 9438208 | tf_op jit(solution)/shard_map/while/body/eval_jaxpr/dot_general | solution.py:153
  69.2 13.2 %fusion.221 = bf16[2048,256]{0,1:T(8,128)(2,1)S(1)} fusion(bf16[2048,2048]{1,0:T(8,128)(2,1)} %get-tuple-element.359, s32[256]{0:T(256)S(1)} %iota_add_fusion.6), kind=kOutput, calls=%fused_computation.14.clone.1 | convolution fusion | flops 2156396544 | bytes 9438208 | tf_op jit(solution)/shard_map/while/body/eval_jaxpr/dot_general | solution.py:152
  84.6 13.2 %fusion.220 = bf16[2048,256]{0,1:T(8,128)(2,1)S(1)} fusion(bf16[2048,2048]{1,0:T(8,128)(2,1)} %get-tuple-element.359, s32[256]{0:T(256)S(1)} %iota_add_fusion.6), kind=kOutput, calls=%fused_computation.13.clone.1 | convolution fusion | flops 2156920832 | bytes 9438208 | tf_op jit(solution)/shard_map/while/body/eval_jaxpr/dot_general | solution.py:153
  98.4 13.2 %fusion.221 = bf16[2048,256]{0,1:T(8,128)(2,1)S(1)} fusion(bf16[2048,2048]{1,0:T(8,128)(2,1)} %get-tuple-element.359, s32[256]{0:T(256)S(1)} %iota_add_fusion.6), kind=kOutput, calls=%fused_computation.14.clone.1 | convolution fusion | flops 2156396544 | bytes 9438208 | tf_op jit(solution)/shard_map/while/body/eval_jaxpr/dot_general | solution.py:152
  113.7 13.2 %fusion.220 = bf16[2048,256]{0,1:T(8,128)(2,1)S(1)} fusion(bf16[2048,2048]{1,0:T(8,128)(2,1)} %get-tuple-element.359, s32[256]{0:T(256)S(1)} %iota_add_fusion.6), kind=kOutput, calls=%fused_computation.13.clone.1 | convolution fusion | flops 2156920832 | bytes 9438208 | tf_op jit(solution)/shard_map/while/body/eval_jaxpr/dot_general | solution.py:153
  127.5 13.2 %fusion.221 = bf16[2048,256]{0,1:T(8,128)(2,1)S(1)} fusion(bf16[2048,2048]{1,0:T(8,128)(2,1)} %get-tuple-element.359, s32[256]{0:T(256)S(1)} %iota_add_fusion.6), kind=kOutput, calls=%fused_computation.14.clone.1 | convolution fusion | flops 2156396544 | bytes 9438208 | tf_op jit(solution)/shard_map/while/body/eval_jaxpr/dot_general | solution.py:152
  142.9 13.2 %fusion.220 = bf16[2048,256]{0,1:T(8,128)(2,1)S(1)} fusion(bf16[2048,2048]{1,0:T(8,128)(2,1)} %get-tuple-element.359, s32[256]{0:T(256)S(1)} %iota_add_fusion.6), kind=kOutput, calls=%fused_computation.13.clone.1 | convolution fusion | flops 2156920832 | bytes 9438208 | tf_op jit(solution)/shard_map/while/body/eval_jaxpr/dot_general | solution.py:153
  156.7 13.2 %fusion.221 = bf16[2048,256]{0,1:T(8,128)(2,1)S(1)} fusion(bf16[2048,2048]{1,0:T(8,128)(2,1)} %get-tuple-element.359, s32[256]{0:T(256)S(1)} %iota_add_fusion.6), kind=kOutput, calls=%fused_computation.14.clone.1 | convolution fusion | flops 2156396544 | bytes 9438208 | tf_op jit(solution)/shard_map/while/body/eval_jaxpr/dot_general | solution.py:152
  172.1 4.5 dynamic-slice_bitcast_fusion.3
  186.0 38.5 %collective-permute-done = bf16[2,64,8,1024]{3,1,2,0:T(8,128)(2,1)S(1)} collective-permute-done((bf16[2,64,8,1024]{3,1,2,0:T(8,128)(2,1)S(1)}, bf16[2,64,8,1024]{3,1,2,0:T(8,128)(2,1)S(1)}, u32[]{:S(2)}, u32[]{:S(2)}) %collective-permute-start) | collective-permute-done | bytes 2097184 | tf_op jit(solution)/shard_map/ppermute | solution.py:34
  224.5 4.2 collective-permute-done.1
  228.7 42.7 %collective-permute-done.2 = bf16[2,64,8,1024]{3,1,2,0:T(8,128)(2,1)S(1)} collective-permute-done((bf16[2,64,8,1024]{3,1,2,0:T(8,128)(2,1)S(1)}, bf16[2,64,8,1024]{3,1,2,0:T(8,128)(2,1)S(1)}, u32[]{:S(2)}, u32[]{:S(2)}) %collective-permute-start.2) | collective-permute-done | bytes 2097184 | tf_op jit(solution)/shard_map/ppermute | solution.py:34
  272.4 3.8 fusion.195
  276.3 5.0 gather_fusion.4
  281.3 4.9 gather_fusion.5
  286.2 8.2 maximum_bitcast_fusion
  294.4 11.9 %copy.128 = bf16[2,4,64,8,1024]{4,3,2,1,0:T(8,128)(2,1)} copy(bf16[2,4,64,8,1024]{4,2,3,0,1:T(8,128)(2,1)} %maximum_bitcast_fusion) | data formatting | bytes 16777216 | tf_op jit(solution)/shard_map/transpose | solution.py:23
  306.3 13.4 %copy.129 = bf16[2,256,8,1024]{1,2,0,3:T(8,128)(2,1)} copy(bf16[2,256,8,1024]{3,2,1,0:T(8,128)(2,1)} %bitcast.177) | data formatting | bytes 16777216 | tf_op jit(solution)/shard_map/reshape | solution.py:25
  319.7 5.8 all-to-all-start
  326.0 4.5 gather_fusion.2
  330.6 4.1 gather_fusion.3
  337.2 3.7 broadcast_select_fusion
  342.6 167.2 %all-to-all-done = bf16[2,256,8,1024]{1,2,0,3:T(8,128)(2,1)} async-done(((bf16[2,256,8,1024]{1,2,0,3:T(8,128)(2,1)}), bf16[2,256,8,1024]{1,2,0,3:T(8,128)(2,1)}, u32[]{:S(2)}, u32[]{:S(2)}) %all-to-all-start) | async-done | bytes 8388640 | tf_op jit(solution)/shard_map/all_to_all | solution.py:169
  509.8 15.9 %copy.131 = bf16[2,4,256,8,256]{4,3,2,1,0:T(8,128)(2,1)} copy(bf16[2,4,256,8,256]{2,3,0,4,1:T(8,128)(2,1)} %bitcast.30) | data formatting | bytes 16777216 | tf_op jit(solution)/shard_map/all_to_all | solution.py:169
  525.8 13.1 %gather_fusion.1 = bf16[1024,2,8,256]{3,2,1,0:T(8,128)(2,1)} fusion(bf16[2,1024,8,256]{3,2,1,0:T(8,128)(2,1)} %bitcast.175, s32[1024]{0:T(1024)S(1)} %broadcast_clamp_fusion.1), kind=kCustom, calls=%fused_computation.1 | custom fusion | bytes 16781312 | tf_op jit(solution)/shard_map/jit(_take)/gather | solution.py:177
  538.8 6.1 select_bitcast_fusion
  544.9 4.9 fusion.54
  549.8 7.4 stack.64
  557.1 7.6 stack.65
  564.8 13.7 %fusion.68 = f32[2,2,4,128,2048]{4,3,2,1,0:T(8,128)} fusion(bf16[1,4,256,2048]{3,2,0,1:T(8,128)(2,1)} %stack.65, bf16[1,4,256,2048]{3,2,0,1:T(8,128)(2,1)} %stack.64, bf16[256,1,2,2,128]{0,4,1,3,2:T(8,128)(2,1)S(1)} %get-tuple-element.267, bf16[256,1,2,2,128]{0,4,1,3,2:T(8,128)(2,1)S(1)} %get-tuple-element.266), kind=kOutput, calls=%fused_computation.108 | convolution fusion | flops 4312793088 | bytes 25690112 | tf_op jit(solution)/shard_map/rcnq,nrsah->sachq/dot_general | solution.py:186
  578.5 6.5 slice_bitcast_fusion.1
  585.0 18.4 %fusion.60 = f32[2,128,2048,4]{2,3,1,0:T(4,128)} fusion(f32[2,4,128,2048]{3,2,1,0:T(8,128)S(1)} %get-tuple-element.255), kind=kOutput, calls=%fused_computation.100 | convolution fusion | flops 100663520 | bytes 16777216 | tf_op jit(solution)/shard_map/ec,lchq->lehq/dot_general | solution.py:87
  603.4 18.7 %fusion.62 = f32[2,128,2048,4]{2,3,1,0:T(4,128)} fusion(f32[2,4,128,2048]{3,2,1,0:T(8,128)S(1)} %get-tuple-element.255), kind=kOutput, calls=%fused_computation.102 | convolution fusion | flops 100663520 | bytes 16777216 | tf_op jit(solution)/shard_map/ec,lchq->lehq/dot_general | solution.py:86
  622.1 18.4 %fusion.64 = f32[2,128,2048,4]{2,3,1,0:T(4,128)} fusion(f32[2,4,128,2048]{3,2,1,0:T(8,128)S(1)} %get-tuple-element.254), kind=kOutput, calls=%fused_computation.104 | convolution fusion | flops 100663520 | bytes 16777216 | tf_op jit(solution)/shard_map/ec,lchq->lehq/dot_general | solution.py:89
  640.5 30.1 %multiply_bitcast_fusion = f32[2,4,128,2048]{3,1,2,0:T(4,128)} fusion(f32[2,128,2048,4]{2,3,1,0:T(4,128)} %fusion.60, f32[2,128,2048,4]{2,3,1,0:T(4,128)} %fusion.64, f32[2,128,2048,4]{2,3,1,0:T(4,128)} %fusion.62, f32[2,4,128,2048]{3,2,1,0:T(8,128)} %copy-done.2), kind=kOutput, calls=%fused_computation.99 | convolution fusion | flops 113246432 | bytes 41943040 | tf_op jit(solution)/shard_map/ec,lchq->lehq/dot_general | solution.py:84
  670.7 11.5 %copy.136 = f32[2,4,128,2048]{3,2,1,0:T(8,128)} copy(f32[2,4,128,2048]{3,1,2,0:T(4,128)} %multiply_bitcast_fusion) | data formatting | bytes 16777216 | tf_op jit(solution)/shard_map/mul | solution.py:90
  682.2 97.7 %reduce-scatter.2.cloned.1.call-done = f32[1,4,128,2048]{3,2,1,0:T(8,128)} async-done(((f32[2,4,128,2048]{3,2,1,0:T(8,128)}), f32[1,4,128,2048]{3,2,1,0:T(8,128)}) %reduce-scatter.2.cloned.1.call-update) | async-done | bytes 4194320 | tf_op jit(solution)/shard_map/reduce_scatter | solution.py:190
  783.1 28.2 %all_to_all.45 = bf16[512,8,256]{2,1,0:T(8,128)(2,1)S(1)} all-to-all(bf16[512,8,256]{2,1,0:T(8,128)(2,1)S(1)} %bitcast.182), channel_id=1, replica_groups=mesh['grp'=4,'mem'=4,'pair'=2] {'grp'}, dimensions={0} | all-to-all | bytes 4194304 | tf_op jit(solution)/shard_map/all_to_all | solution.py:193
  812.9 4.6 all-to-all-start.2
  817.7 2.8 gather_fusion
  820.9 44.4 %all-to-all-done.2 = bf16[128,32,256]{2,1,0:T(8,128)(2,1)S(1)} async-done(((bf16[128,32,256]{2,1,0:T(8,128)(2,1)}), bf16[128,32,256]{2,1,0:T(8,128)(2,1)S(1)}, u32[]{:S(2)}, u32[]{:S(2)}) %all-to-all-start.2) | async-done | bytes 2097184 | tf_op jit(solution)/shard_map/all_to_all | solution.py:192
  866.7 4.1 fusion.75
  870.8 5.1 convert_bitcast_fusion
  875.9 88.8 %while.30 = (s32[]{:T(128)}, f32[4,32,8,32]{1,3,2,0:T(8,128)S(1)}, f32[4,32,8,32]{1,3,2,0:T(8,128)S(1)}, s32[4]{0:T(128)S(1)}, s32[32,1024]{1,0:T(8,128)S(1)}, /...) while((s32[]{:T(128)}, f32[4,32,8,32]{1,3,2,0:T(8,128)S(1)}, ...), condition=%wide.region_5.6_spmd, body=%wide.region_4.5_spmd.sunk | while | flops 83378192 | bytes 5309699 | solution.py:131
  880.9 4.4 fusion.228
  885.3 4.3 fusion.229
  889.6 4.3 fusion.226
  893.9 4.4 fusion.227
  903.1 4.4 fusion.228
  907.5 4.3 fusion.229
  911.8 4.3 fusion.226
  916.1 4.4 fusion.227
  925.3 4.4 fusion.228
  929.7 4.3 fusion.229
  934.0 4.3 fusion.226
  938.3 4.4 fusion.227
  947.4 4.4 fusion.228
  951.8 4.3 fusion.229
  956.0 4.3 fusion.226
  960.3 4.4 fusion.227
  (90 shorter events, 47.4 us)
Async XLA Ops:
  6.5 324.0 %copy-start = (f32[64,2,256]{2,1,0:T(2,128)S(1)}, f32[64,2,256]{2,1,0:T(2,128)}, u32[]{:S(2)}) copy-start(f32[64,2,256]{2,1,0:T(2,128)} %param.11) | copy-start | bytes 393220
  177.7 46.8 %collective-permute-start = (bf16[2,64,8,1024]{3,1,2,0:T(8,128)(2,1)S(1)}, bf16[2,64,8,1024]{3,1,2,0:T(8,128)(2,1)S(1)}, u32[]{:S(2)}, u32[]{:S(2)}) collective-permute-start(bf16[2,64,8,1024]{3,1,2,0:T(8,128)(2,1)S(1)} %copy.124), channel_id=1, source_target_pairs={{0,8},{8,16},{16,24},{24,0},{1,9},{9,17},{17,25},{25,1},{2,10},{10... | collective-permute-start | bytes 6291464 | tf_op jit(solution)/shard_map/ppermute | solution.py:34
  179.6 49.0 %collective-permute-start.1 = (bf16[2,64,8,1024]{3,1,2,0:T(8,128)(2,1)S(1)}, bf16[2,64,8,1024]{3,1,2,0:T(8,128)(2,1)S(1)}, u32[]{:S(2)}, u32[]{:S(2)}) collective-permute-start(bf16[2,64,8,1024]{3,1,2,0:T(8,128)(2,1)S(1)} %copy.125), channel_id=1, source_target_pairs={{0,16},{8,24},{16,0},{24,8},{1,17},{9,25},{17,1},{25,9},{2,18},{10... | collective-permute-start | bytes 6291464 | tf_op jit(solution)/shard_map/ppermute | solution.py:34
  183.3 88.0 %collective-permute-start.2 = (bf16[2,64,8,1024]{3,1,2,0:T(8,128)(2,1)S(1)}, bf16[2,64,8,1024]{3,1,2,0:T(8,128)(2,1)S(1)}, u32[]{:S(2)}, u32[]{:S(2)}) collective-permute-start(bf16[2,64,8,1024]{3,1,2,0:T(8,128)(2,1)S(1)} %copy.126), channel_id=1, source_target_pairs={{0,24},{8,0},{16,8},{24,16},{1,25},{9,1},{17,9},{25,17},{2,26},{10... | collective-permute-start | bytes 6291464 | tf_op jit(solution)/shard_map/ppermute | solution.py:34
  319.7 6.2 copy-start.8
  319.7 6.3 copy-start.6
  319.7 190.1 %all-to-all-start = ((bf16[2,256,8,1024]{1,2,0,3:T(8,128)(2,1)}), bf16[2,256,8,1024]{1,2,0,3:T(8,128)(2,1)}, u32[]{:S(2)}, u32[]{:S(2)}) async-start(bf16[2,256,8,1024]{1,2,0,3:T(8,128)(2,1)} %copy.129), calls=%async_computation | async-start | bytes 16777216 | tf_op jit(solution)/shard_map/all_to_all | solution.py:169
  325.5 454.4 %reduce-scatter.2.cloned.1.call-start = ((), (), s32[]{:S(2)}) async-start(), calls=%async_computation.4 | async-start | bytes 12582912 | tf_op jit(solution)/shard_map/reduce_scatter | solution.py:190
  584.9 37.2 %copy-start.2 = (f32[2,4,128,2048]{3,2,1,0:T(8,128)}, f32[2,4,128,2048]{3,2,1,0:T(8,128)S(1)}, u32[]{:S(2)}) copy-start(f32[2,4,128,2048]{3,2,1,0:T(8,128)S(1)} %get-tuple-element.254) | copy-start | bytes 25165828
  811.3 6.2 copy-start.5
  811.3 6.4 copy-start.7
  812.9 52.4 %all-to-all-start.2 = ((bf16[128,32,256]{2,1,0:T(8,128)(2,1)}), bf16[128,32,256]{2,1,0:T(8,128)(2,1)S(1)}, u32[]{:S(2)}, u32[]{:S(2)}) async-start(bf16[128,32,256]{2,1,0:T(8,128)(2,1)} %bitcast.181), calls=%async_computation.3 | async-start | bytes 4194304 | tf_op jit(solution)/shard_map/all_to_all | solution.py:192
  870.8 5.1 copy-start.3
  870.8 5.1 copy-start.4
  964.7 3.2 copy-start.1
Sparse Core Ops, SparseCore 0:
  682.3 97.5 reduce-scatter.1
